TPU v7x, 256 devices: a whole 4x4x8 slice. The times are simulated.
256 devices in a mesh: tensor: 8 (over z_hi, core), mirror: 2 (over z_lo), dp: 16 (over x, y).
Axes of the slice: x: 4, y: 4, z: 8 (z_hi: 4, z_lo: 2; z = z_hi * 2 + z_lo), core: 2. Of those that a mesh axis runs over, the one named last changes fastest.
Arguments:
- layer_input: bfloat16 [32, 256, 4096], P(('mirror', 'dp'), 'tensor'), may hold values from -6 to 6
- qk_weight: bfloat16 [4096, 2, 4096], P(None, None, 'tensor'), may hold values from -0.09375 to 0.09375
- query_proj: bfloat16 [32, 256, 4096], P(('mirror', 'dp'), None, 'tensor'), may hold values from -24 to 24
- key_proj: bfloat16 [32, 256, 4096], P(('mirror', 'dp'), None, 'tensor'), may hold values from -24 to 24
- value_proj: bfloat16 [32, 256, 4096], P(('mirror', 'dp'), None, 'tensor'), may hold values from -6 to 6
- head_grad: bfloat16 [32, 256, 4096], P(('mirror', 'dp'), None, 'tensor'), may hold values from -6 to 6
- doc_ids: int32 [32, 256], P(('mirror', 'dp')), may hold values from 0 to 3, as said below
Outputs:
- input_grad: bfloat16 [32, 256, 4096], P(('mirror', 'dp'), 'tensor')
- qk_weight_grad: float32 [4096, 2, 4096], P(('mirror', 'dp'), None, 'tensor')
Inputs may be any that keep to these rules, and one draw needn't show every extreme that they name: `doc_ids`: within each sequence of 128 tokens the ids start at 0, never fall, and each of the four documents holds a multiple of 8 tokens.
All inputs are finite; a program needn't handle non-finite values.
Results may differ from a plain program's by a relative error of at most 0.023.
Values may be sent and summed in bfloat16 or wider, within the bound.
A program may use at most 128 MiB of HBM per device.

v0:
```python
import math

import jax
import jax.numpy as jnp
from jax import lax
from jax.sharding import PartitionSpec as P

HD = 128
SEQ = 128


def rotate_pairs(values, cosine, sine_table):
    half = values.shape[-1] // 2
    first_half = values[..., :half]
    second_half = values[..., half:]
    cos_b = cosine[None, :, None, :]
    sin_b = sine_table[None, :, None, :]
    return jnp.concatenate(
        [first_half * cos_b - second_half * sin_b, second_half * cos_b + first_half * sin_b],
        axis=-1,
    )


def unrotate_pairs(values, cosine, sine_table):
    half = values.shape[-1] // 2
    first_half = values[..., :half]
    second_half = values[..., half:]
    cos_b = cosine[None, :, None, :]
    sin_b = sine_table[None, :, None, :]
    return jnp.concatenate(
        [first_half * cos_b + second_half * sin_b, second_half * cos_b - first_half * sin_b],
        axis=-1,
    )


def attention_grads(query_rows, key_rows, value_rows, grad_rows, doc_row):
    token_count, full_width = query_rows.shape
    head_count = full_width // HD
    micro_count = token_count // SEQ
    shape_four = (micro_count, SEQ, head_count, HD)
    positions = jnp.arange(SEQ).astype(jnp.float32)
    inverse = jnp.exp(-(2.0 * jnp.arange(HD // 2).astype(jnp.float32) / HD) * math.log(10000.0))
    angles = positions[:, None] * inverse[None, :]
    cosine = jnp.cos(angles)
    sine_table = jnp.sin(angles)
    q_rot = rotate_pairs(
        query_rows.reshape(shape_four).astype(jnp.float32), cosine, sine_table
    ).astype(jnp.bfloat16)
    k_rot = rotate_pairs(
        key_rows.reshape(shape_four).astype(jnp.float32), cosine, sine_table
    ).astype(jnp.bfloat16)
    scale = 1.0 / math.sqrt(HD)
    scores = jnp.einsum("bshd,bthd->bhst", q_rot, k_rot, preferred_element_type=jnp.float32) * scale
    docs = doc_row.reshape(micro_count, SEQ)
    index_seq = jnp.arange(SEQ)
    causal = index_seq[None, :] <= index_seq[:, None]
    allowed = causal[None, :, :] & (docs[:, :, None] == docs[:, None, :])
    scores = jnp.where(allowed[:, None, :, :], scores, -1e30)
    highest = jnp.max(scores, axis=-1, keepdims=True)
    exps = jnp.exp(scores - highest)
    probs = exps / jnp.sum(exps, axis=-1, keepdims=True)
    dprob = jnp.einsum(
        "bshd,bthd->bhst",
        grad_rows.reshape(shape_four),
        value_rows.reshape(shape_four),
        preferred_element_type=jnp.float32,
    )
    delta = jnp.sum(probs * dprob, axis=-1, keepdims=True)
    dscore = (probs * (dprob - delta)).astype(jnp.bfloat16)
    dq_rot = (
        jnp.einsum("bhst,bthd->bshd", dscore, k_rot, preferred_element_type=jnp.float32) * scale
    )
    dk_rot = (
        jnp.einsum("bhst,bshd->bthd", dscore, q_rot, preferred_element_type=jnp.float32) * scale
    )
    query_grad = (
        unrotate_pairs(dq_rot, cosine, sine_table)
        .astype(jnp.bfloat16)
        .reshape(token_count, full_width)
    )
    key_grad = (
        unrotate_pairs(dk_rot, cosine, sine_table)
        .astype(jnp.bfloat16)
        .reshape(token_count, full_width)
    )
    return (query_grad, key_grad)


def shards(layer_input, qk_weight, query_proj, key_proj, value_proj, head_grad, doc_ids):
    tensor_count = lax.axis_size("tensor")
    mirror_count = lax.axis_size("mirror")
    data_count = lax.axis_size("dp")
    replicas = mirror_count * data_count
    token_count = query_proj.shape[1]
    group_width = query_proj.shape[2]
    model_width = layer_input.shape[2]
    block_rows = model_width // replicas
    query_grad, key_grad = attention_grads(
        query_proj[0], key_proj[0], value_proj[0], head_grad[0], doc_ids[0]
    )
    grad_pair = jnp.concatenate([query_grad, key_grad], axis=1)
    weight_flat = qk_weight.reshape(model_width, 2 * group_width)
    summed_input = lax.psum_scatter(
        lax.dot_general(
            grad_pair, weight_flat, (((1,), (1,)), ((), ())), preferred_element_type=jnp.float32
        ).astype(jnp.bfloat16),
        "tensor",
        scatter_dimension=0,
        tiled=True,
    )
    input_grad = summed_input.reshape(1, token_count // tensor_count, model_width)
    gathered = lax.all_gather(layer_input, "tensor", axis=1, tiled=True)[0]
    summed = lax.psum_scatter(
        lax.dot_general(
            gathered, grad_pair, (((0,), (0,)), ((), ())), preferred_element_type=jnp.float32
        ).astype(jnp.bfloat16),
        ("mirror", "dp"),
        scatter_dimension=0,
        tiled=True,
    ).astype(jnp.float32)
    weight_grad = (summed / replicas).reshape(block_rows, 2, group_width)
    return (input_grad, weight_grad)


def solution(mesh):
    in_specs = (
        P(("mirror", "dp"), "tensor", None),
        P(None, None, "tensor"),
        P(("mirror", "dp"), None, "tensor"),
        P(("mirror", "dp"), None, "tensor"),
        P(("mirror", "dp"), None, "tensor"),
        P(("mirror", "dp"), None, "tensor"),
        P(("mirror", "dp"), None),
    )
    out_specs = (P(("mirror", "dp"), "tensor", None), P(("mirror", "dp"), None, "tensor"))
    return jax.shard_map(shards, mesh=mesh, in_specs=in_specs, out_specs=out_specs, check_vma=False)
```

profile of v0, /device:TPU:1, one launch (start us, length us, event | category | flops | bytes accessed | tf_op | source)
XLA Modules:
  0.0 300.0 jit_solution(3463841190845136703)
XLA Ops:
  7.2 0.0 all-gather.2.cloned.1.call-start
  7.2 0.7 all-gather.2.cloned.1.call-update
  7.9 0.0 reduce-scatter.7.cloned.1.call-start
  7.9 1.1 reshape.110
  9.1 1.1 reshape.111
  10.2 1.0 reshape_squeeze.9
  11.2 1.0 reshape_squeeze.8
  12.3 0.9 compare_and_fusion
  13.1 0.3 multiply_cosine_fusion
  13.4 0.6 fusion.18
  14.1 0.3 subtract_convert_fusion.3
  14.4 0.5 fusion.20
  14.9 0.3 multiply_reduce_fusion
  15.2 0.1 multiply_convert_fusion
  15.3 0.3 fusion.4
  15.6 0.4 fusion.5
  15.9 0.5 add_convert_fusion
  16.4 0.1 pad_maximum_fusion.2
  16.6 0.2 copy.42
  16.8 0.1 pad_maximum_fusion.3
  16.9 0.2 copy.46
  17.2 32.9 %all-gather.2.cloned.1.call-done = bf16[1,256,4096]{2,1,0:T(8,128)(2,1)} async-done(((bf16[1,32,4096]{2,1,0:T(8,128)(2,1)}), bf16[1,256,4096]{2,1,0:T(8,128)(2,1)}) %all-gather.2.cloned.1.call-update) | async-done | bytes 2097168 | tf_op jit(solution)/shard_map/all_gather | solution.py:112
  50.2 7.2 %convert_bitcast_fusion = bf16[4096,1024]{0,1:T(8,128)(2,1)} fusion(bf16[256,1024]{1,0:T(8,128)(2,1)S(1)} %bitcast_dynamic-update-slice_fusion, bf16[1,256,4096]{2,1,0:T(8,128)(2,1)} %all-gather.2.cloned.1.call-done), kind=kOutput, calls=%fused_computation.1 | convolution fusion | flops 2151677952 | bytes 11010048 | tf_op jit(solution)/shard_map/dot_general | solution.py:114
  57.4 12.0 %copy.54 = bf16[4096,1024]{1,0:T(8,128)(2,1)} copy(bf16[4096,1024]{0,1:T(8,128)(2,1)} %convert_bitcast_fusion) | data formatting | bytes 16777216
  69.3 0.0 reduce-scatter.7.cloned.1.call-update
  69.4 0.2 reduce-scatter.5.cloned.1.call-start
  69.6 9.3 %copy.62 = bf16[512,8,2,512]{3,1,2,0:T(8,128)(2,1)} copy(bf16[512,8,2,512]{3,2,1,0:T(2,128)(2,1)} %bitcast.28) | data formatting | bytes 16777216
  78.9 7.1 %convolution_convert_fusion = bf16[256,4096]{1,0:T(8,128)(2,1)} fusion(bf16[256,1024]{1,0:T(8,128)(2,1)S(1)} %bitcast_dynamic-update-slice_fusion, bf16[4096,1024]{1,0:T(8,128)(2,1)} %bitcast.29), kind=kOutput, calls=%fused_computation.2 | convolution fusion | flops 2148532224 | bytes 11010048 | tf_op jit(solution)/shard_map/dot_general | solution.py:104
  86.0 0.0 reduce-scatter.5.cloned.1.call-update
  86.0 143.3 %reduce-scatter.7.cloned.1.call-done = bf16[128,1024]{1,0:T(8,128)(2,1)} async-done(((bf16[4096,1024]{1,0:T(8,128)(2,1)}), bf16[128,1024]{1,0:T(8,128)(2,1)}) %reduce-scatter.7.cloned.1.call-update) | async-done | bytes 262160
  229.4 1.1 copy.55
  230.5 1.0 copy.47
  231.5 61.9 %reduce-scatter.5.cloned.1.call-done = bf16[32,4096]{1,0:T(8,128)(2,1)} async-done(((bf16[256,4096]{1,0:T(8,128)(2,1)}), bf16[32,4096]{1,0:T(8,128)(2,1)}) %reduce-scatter.5.cloned.1.call-update) | async-done | bytes 262160 | tf_op jit(solution)/shard_map/reduce_scatter | solution.py:103
  (6 shorter events, 0.1 us)
Async XLA Ops:
  7.2 43.0 %all-gather.2.cloned.1.call-start = ((), (), s32[]{:S(2)}) async-start(), calls=%async_computation.3 | async-start | bytes 2359296 | tf_op jit(solution)/shard_map/all_gather | solution.py:112
  7.9 221.5 %reduce-scatter.7.cloned.1.call-start = ((), (), s32[]{:S(2)}) async-start(), calls=%async_computation.4 | async-start | bytes 8650752
  69.4 224.1 %reduce-scatter.5.cloned.1.call-start = ((), (), s32[]{:S(2)}) async-start(), calls=%async_computation.2 | async-start | bytes 2359296 | tf_op jit(solution)/shard_map/reduce_scatter | solution.py:103
Sparse Core Ops, SparseCore 0:
  9.8 40.2 all-gather.1
  69.5 159.8 reduce-scatter.6
  232.5 60.9 reduce-scatter.4
where the time goes:
time: 302 us; the launch traced here: 300 us
  waiting for transfers between devices  239 us (79%)
  local copies, waits for them, and re-layouts  28.7 us (10%)
  matrix products  15.8 us (5%)
  between operations  13.9 us (5%)
    unnamed x4, waiting for transfers between devices  144 us
    reduce_scatter x1, waiting for transfers between devices, shards(): lax.psum_scatter(lax.dot_general(grad_pair, weight_flat, (((1,), (1,)), (...  61.9 us
    all_gather x1, waiting for transfers between devices, shards(): gathered = lax.all_gather(layer_input, 'tensor', axis=1, tiled=True)[0]  32.9 us
    unnamed x5, local copies, waits for them, and re-layouts  23.4 us
    dot_general x1, matrix products, shards(): lax.dot_general(gathered, grad_pair, (((0,), (0,)), ((), ())), preferred_...  7.19 us
    dot_general x1, matrix products, shards(): lax.dot_general(grad_pair, weight_flat, (((1,), (1,)), ((), ())), preferr...  7.12 us
  transfers between devices with their start and end apart: 3, of which 3 were waited for; matrix products, arithmetic and copies ran while one was open for 9% of the time, Pallas kernels for 0%

commit v1 on v0

v1 whole, which is shorter than its diff:
```python
import functools
import math

import jax
import jax.numpy as jnp
import numpy as np
from jax import lax
from jax.experimental import pallas as pl
from jax.experimental.pallas import tpu as pltpu
from jax.sharding import PartitionSpec as P

HD = 128
SEQ = 128
MESH = pl.DeviceIdType.MESH
NT = (((1,), (1,)), ((), ()))
TN = (((0,), (0,)), ((), ()))
BF16 = jnp.bfloat16
F32 = jnp.float32
COPIES = 96


def rope_tables():
    positions = np.arange(SEQ).astype(np.float32)
    inverse = np.exp(
        -(np.float32(2.0) * np.arange(HD // 2).astype(np.float32) / np.float32(HD))
        * np.float32(math.log(10000.0))
    )
    angles = positions[:, None] * inverse[None, :].astype(np.float32)
    cosine = np.cos(angles).astype(np.float32)
    sine = np.sin(angles).astype(np.float32)
    return (
        np.concatenate([cosine, cosine], axis=1),
        np.concatenate([-sine, sine], axis=1),
    )


def kernel(
    x_ref, w_hbm, q_ref, k_ref, v_ref, g_ref, doc_ref, cos_ref, sin_ref,
    ig_ref, wg_ref,
    w_buf, x_buf, g_buf, g_tok, p_buf, p_sib, z_out, z_one, z_two,
    t_buf, r_one, r_two, m_out, m_in,
    w_sem, l_sem, send_sem, recv_sem,
):
    t = lax.axis_index("tensor")
    m = lax.axis_index("mirror")
    d = lax.axis_index("dp")
    zh, c = lax.div(t, 2), lax.rem(t, 2)
    x, y = lax.div(d, 4), lax.rem(d, 4)

    def at_z(step):
        return {"tensor": lax.rem(zh + step, 4) * 2 + c}

    def at_x(step):
        return {"dp": lax.rem(x + step, 4) * 4 + y}

    def at_y(step):
        return {"dp": x * 4 + lax.rem(y + step, 4)}

    sibling = {"tensor": zh * 2 + 1 - c}
    twin = {"mirror": 1 - m}

    w_in = [
        pltpu.make_async_copy(w_hbm.at[pl.ds(i * 512, 512)], w_buf.at[i], w_sem.at[i])
        for i in range(8)
    ]
    for copy in w_in:
        copy.start()
    halves = (1 - m, m)
    own_in = [
        pltpu.make_async_copy(
            x_ref.at[0, :, pl.ds(pl.multiple_of(halves[u] * 2048 + x * 512, 512), 512)],
            x_buf.at[u, 0, pl.ds(pl.multiple_of(t * 32, 32), 32)],
            l_sem.at[u],
        )
        for u in range(2)
    ]
    for copy in own_in:
        copy.start()

    barrier = pltpu.get_barrier_semaphore()
    partners = [sibling, at_z(1), at_z(3), at_x(1), at_x(2), at_x(3), at_y(1), at_y(3), twin]
    for partner in partners:
        pl.semaphore_signal(barrier, inc=1, device_id=partner, device_id_type=MESH)
    pl.semaphore_wait(barrier, len(partners))

    sent = []

    def send(src, dst, device):
        index = len(sent)
        copy = pltpu.make_async_remote_copy(
            src_ref=src,
            dst_ref=dst,
            send_sem=send_sem.at[index],
            recv_sem=recv_sem.at[index],
            device_id=device,
            device_id_type=MESH,
        )
        copy.start()
        sent.append(copy)
        return copy

    turned = []
    for u in range(2):
        for step in (1, 3, 2):
            column = pl.multiple_of(halves[u] * 2048 + lax.rem(x + step, 4) * 512, 512)
            turned.append(
                send(
                    x_ref.at[0, :, pl.ds(column, 512)],
                    x_buf.at[u, 4 - step, pl.ds(pl.multiple_of(t * 32, 32), 32)],
                    at_x(step),
                )
            )

    def piece(which, zi, half=None):
        start = (lax.rem(zi, 4) * 2 + c) * 32
        if half is None:
            rows = pl.ds(pl.multiple_of(start, 32), 32)
        else:
            rows = pl.ds(pl.multiple_of(start + 16 * half, 16), 16)
        if which == 0:
            return x_buf.at[:, 0, rows]
        return x_buf.at[which - 1, pl.ds(1, 3), rows]

    ring = {}

    def x_start(which):
        own = piece(which, zh)
        ring[which] = [send(own, own, at_z(1)), send(own, own, at_z(3))]
        ring[which, "sib"] = [send(own, own, sibling)]

    def x_forward(which):
        up, down = ring[which]
        up.wait_recv()
        half = piece(which, zh + 3, 0)
        fu = send(half, half, at_z(1))
        whole = piece(which, zh + 3)
        s_up = send(whole, whole, sibling)
        down.wait_recv()
        half = piece(which, zh + 1, 1)
        fd = send(half, half, at_z(3))
        whole = piece(which, zh + 1)
        s_down = send(whole, whole, sibling)
        ring[which, "far"] = [fu, fd]
        ring[which, "sib"] += [s_up, s_down]

    def x_far(which):
        fu, fd = ring[which, "far"]
        fu.wait_recv()
        half = piece(which, zh + 2, 0)
        s_up = send(half, half, sibling)
        fd.wait_recv()
        half = piece(which, zh + 2, 1)
        s_down = send(half, half, sibling)
        ring[which, "sib"] += [s_up, s_down]

    def x_finish(which):
        for copy in ring[which, "sib"]:
            copy.wait_recv()

    for copy in own_in:
        copy.wait()
    x_start(0)

    cosine, sine = cos_ref[...], sin_ref[...]
    scale = 1.0 / math.sqrt(HD)
    row = lax.broadcasted_iota(jnp.int32, (SEQ, SEQ), 0)
    col = lax.broadcasted_iota(jnp.int32, (SEQ, SEQ), 1)
    allowed = []
    for s in range(2):
        docs = jnp.broadcast_to(doc_ref[:, s * SEQ : (s + 1) * SEQ].astype(F32), (SEQ, SEQ))
        allowed.append((col <= row) & (docs == docs.T))

    def rotate(values):
        return values * cosine + pltpu.roll(values, 64, 1) * sine

    def unrotate(values):
        return values * cosine - pltpu.roll(values, 64, 1) * sine

    def heads(pair):
        for s in range(2):
            rows = slice(s * SEQ, (s + 1) * SEQ)
            for j in range(2):
                h = 2 * pair + j
                cols = slice(h * HD, (h + 1) * HD)
                q_rot = rotate(q_ref[0, rows, cols].astype(F32)).astype(BF16)
                k_rot = rotate(k_ref[0, rows, cols].astype(F32)).astype(BF16)
                scores = lax.dot_general(q_rot, k_rot, NT, preferred_element_type=F32) * scale
                scores = jnp.where(allowed[s], scores, -1e30)
                exps = jnp.exp(scores - jnp.max(scores, axis=-1, keepdims=True))
                probs = exps / jnp.sum(exps, axis=-1, keepdims=True)
                dprob = lax.dot_general(
                    g_ref[0, rows, cols], v_ref[0, rows, cols], NT, preferred_element_type=F32
                )
                delta = jnp.sum(probs * dprob, axis=-1, keepdims=True)
                dscore = (probs * (dprob - delta)).astype(BF16)
                dq = jnp.dot(dscore, k_rot, preferred_element_type=F32) * scale
                dk = lax.dot_general(dscore, q_rot, TN, preferred_element_type=F32) * scale
                dq, dk = unrotate(dq), unrotate(dk)
                g_tok[rows, h * HD : (h + 1) * HD] = dq.astype(BF16)
                g_tok[rows, 512 + h * HD : 512 + (h + 1) * HD] = dk.astype(BF16)
                g_buf[pair, j * 256 : j * 256 + 128, rows] = dq.T.astype(BF16)
                g_buf[pair, j * 256 + 128 : j * 256 + 256, rows] = dk.T.astype(BF16)

    grads = {}

    def g_slot(pair, slot):
        return g_buf.at[pair, :, pl.ds(slot * 256, 256)]

    def g_start(pair):
        grads[pair] = [
            send(g_slot(pair, 0), g_slot(pair, 3), at_x(1)),
            send(g_slot(pair, 0), g_slot(pair, 1), at_x(3)),
        ]

    def g_forward(pair):
        up, down = grads[pair]
        low, high = pl.ds(0, 256), pl.ds(256, 256)
        up.wait_recv()
        fu = send(
            g_buf.at[pair, low, pl.ds(768, 256)], g_buf.at[pair, low, pl.ds(512, 256)], at_x(1)
        )
        down.wait_recv()
        fd = send(
            g_buf.at[pair, high, pl.ds(256, 256)], g_buf.at[pair, high, pl.ds(512, 256)], at_x(3)
        )
        grads[pair, "far"] = [fu, fd]

    def g_finish(pair):
        for copy in grads[pair, "far"]:
            copy.wait_recv()

    pick_row = lax.broadcasted_iota(jnp.int32, (256, 256), 0)
    pick_col = lax.broadcasted_iota(jnp.int32, (256, 256), 1)
    pick = jnp.where(
        pick_col == jnp.where(pick_row < 128, 2 * pick_row, 2 * pick_row - 255), 1.0, 0.0
    ).astype(BF16)
    swaps = {}

    def p_unit(u):
        for i in (2 * u, 2 * u + 1):
            w_in[i].wait()
            mixed = w_buf[i].reshape(1024, 512)
            parts = [
                jnp.dot(pick, mixed[b * 256 : (b + 1) * 256], preferred_element_type=F32).astype(
                    BF16
                )
                for b in range(4)
            ]
            w_q = jnp.concatenate([part[:128] for part in parts], axis=0)
            w_k = jnp.concatenate([part[128:] for part in parts], axis=0)
            partial = lax.dot_general(
                g_tok[:, :512], w_q, NT, preferred_element_type=F32
            ) + lax.dot_general(g_tok[:, 512:], w_k, NT, preferred_element_type=F32)
            off = (i % 2) * 512
            p_buf[u, :, :, :, off : off + 512] = partial.astype(BF16).reshape(4, 2, 32, 512)
        swaps[u] = send(p_buf.at[u, :, 1 - c], p_sib.at[u], sibling)

    def p_sum(u, zi):
        return p_buf[u, zi, c].astype(F32) + p_sib[u, zi].astype(F32)

    def p_one(u):
        swaps[u].wait_recv()
        z_out[u, 0] = p_sum(u, lax.rem(zh + 2, 4)).astype(BF16)
        low, high = pl.ds(0, 16), pl.ds(16, 16)
        swaps[u, 1] = [
            send(z_out.at[u, 0, low], z_one.at[u, 0], at_z(1)),
            send(z_out.at[u, 0, high], z_one.at[u, 1], at_z(3)),
        ]

    def p_two(u):
        up, down = swaps[u, 1]
        up.wait_recv()
        total = p_sum(u, lax.rem(zh + 1, 4))
        z_out[u, 1, :16] = (total[:16] + z_one[u, 0].astype(F32)).astype(BF16)
        z_out[u, 1, 16:] = total[16:].astype(BF16)
        fu = send(z_out.at[u, 1], z_two.at[u, 0], at_z(1))
        down.wait_recv()
        total = p_sum(u, lax.rem(zh + 3, 4))
        z_out[u, 2, :16] = total[:16].astype(BF16)
        z_out[u, 2, 16:] = (total[16:] + z_one[u, 1].astype(F32)).astype(BF16)
        fd = send(z_out.at[u, 2], z_two.at[u, 1], at_z(3))
        swaps[u, 2] = [fu, fd]

    def p_end(u):
        for copy in swaps[u, 2]:
            copy.wait_recv()
        total = p_sum(u, zh) + z_two[u, 0].astype(F32) + z_two[u, 1].astype(F32)
        ig_ref[:, u * 1024 : (u + 1) * 1024] = total.astype(BF16)

    terms = {}

    def t_unit(u, pair):
        term = jnp.dot(g_buf[pair], x_buf[u].reshape(1024, 512), preferred_element_type=F32)
        for b in range(4):
            t_buf[u, pair, b] = term[:, b * 128 : (b + 1) * 128].astype(BF16)
        far = lax.rem(y + 2, 4)
        n = 2 * u + pair
        terms[n] = [
            send(t_buf.at[u, pair, far, pl.ds(0, 256)], r_one.at[n, 0], at_y(1)),
            send(t_buf.at[u, pair, far, pl.ds(256, 256)], r_one.at[n, 1], at_y(3)),
        ]

    def t_two(u, pair):
        n = 2 * u + pair
        up, down = terms[n]
        up.wait_recv()
        b = lax.rem(y + 1, 4)
        t_buf[u, pair, b, :256] = (
            t_buf[u, pair, b, :256].astype(F32) + r_one[n, 0].astype(F32)
        ).astype(BF16)
        fu = send(t_buf.at[u, pair, b], r_two.at[n, 0], at_y(1))
        down.wait_recv()
        b = lax.rem(y + 3, 4)
        t_buf[u, pair, b, 256:] = (
            t_buf[u, pair, b, 256:].astype(F32) + r_one[n, 1].astype(F32)
        ).astype(BF16)
        fd = send(t_buf.at[u, pair, b], r_two.at[n, 1], at_y(3))
        terms[n, 2] = [fu, fd]

    def t_sum(u, pair):
        n = 2 * u + pair
        for copy in terms[n, 2]:
            copy.wait_recv()
        return (
            t_buf[u, pair, y].astype(F32) + r_two[n, 0].astype(F32) + r_two[n, 1].astype(F32)
        )

    def t_away(pair):
        m_out[pair] = t_sum(0, pair).astype(BF16)
        terms["m", pair] = send(m_out.at[pair], m_in.at[pair], twin)

    def t_end(pair):
        total = t_sum(1, pair)
        terms["m", pair].wait_recv()
        total = (total + m_in[pair].astype(F32)) * (1.0 / 32.0)
        for j in range(2):
            for p in range(2):
                block = total[j * 256 + p * 128 : j * 256 + p * 128 + 128]
                at = p * 512 + (2 * pair + j) * 128
                wg_ref[:, at : at + 128] = block.T

    heads(0)
    g_start(0)
    for copy in turned:
        copy.wait_recv()
    x_start(1)
    x_start(2)
    heads(1)
    g_start(1)
    p_unit(0)
    x_forward(0)
    p_unit(1)
    p_unit(2)
    g_forward(0)
    x_forward(1)
    x_far(0)
    p_unit(3)
    x_forward(2)
    g_forward(1)
    x_far(1)
    x_finish(0)
    x_finish(1)
    g_finish(0)
    t_unit(0, 0)
    p_one(0)
    p_one(1)
    t_two(0, 0)
    g_finish(1)
    t_unit(0, 1)
    x_far(2)
    p_one(2)
    p_one(3)
    x_finish(2)
    t_unit(1, 0)
    t_unit(1, 1)
    p_two(0)
    t_two(0, 1)
    t_away(0)
    p_two(1)
    t_two(1, 0)
    t_away(1)
    p_two(2)
    t_two(1, 1)
    p_two(3)
    p_end(0)
    t_end(0)
    p_end(1)
    t_end(1)
    p_end(2)
    p_end(3)
    for copy in sent:
        copy.wait_send()


def shards(layer_input, qk_weight, query_proj, key_proj, value_proj, head_grad, doc_ids):
    cosine, sine = rope_tables()
    vmem = pl.BlockSpec(memory_space=pltpu.VMEM)
    dma = pltpu.SemaphoreType.DMA
    input_grad, weight_grad = pl.pallas_call(
        kernel,
        out_shape=(
            jax.ShapeDtypeStruct((32, 4096), BF16),
            jax.ShapeDtypeStruct((128, 1024), F32),
        ),
        in_specs=[vmem, pl.BlockSpec(memory_space=pl.ANY)] + [vmem] * 7,
        out_specs=(vmem, vmem),
        scratch_shapes=[
            pltpu.VMEM((8, 512, 2, 512), BF16),
            pltpu.VMEM((2, 4, 256, 512), BF16),
            pltpu.VMEM((2, 512, 1024), BF16),
            pltpu.VMEM((256, 1024), BF16),
            pltpu.VMEM((4, 4, 2, 32, 1024), BF16),
            pltpu.VMEM((4, 4, 32, 1024), BF16),
            pltpu.VMEM((4, 3, 32, 1024), BF16),
            pltpu.VMEM((4, 2, 16, 1024), BF16),
            pltpu.VMEM((4, 2, 32, 1024), BF16),
            pltpu.VMEM((2, 2, 4, 512, 128), BF16),
            pltpu.VMEM((4, 2, 256, 128), BF16),
            pltpu.VMEM((4, 2, 512, 128), BF16),
            pltpu.VMEM((2, 512, 128), BF16),
            pltpu.VMEM((2, 512, 128), BF16),
            dma((8,)),
            dma((2,)),
            dma((COPIES,)),
            dma((COPIES,)),
        ],
        compiler_params=pltpu.CompilerParams(
            collective_id=0, has_side_effects=True, vmem_limit_bytes=58 << 20
        ),
        name="qk_backward",
    )(
        layer_input, qk_weight, query_proj, key_proj, value_proj, head_grad, doc_ids,
        jnp.asarray(cosine), jnp.asarray(sine),
    )
    return (input_grad.reshape(1, 32, 4096), weight_grad.reshape(128, 2, 512))


def solution(mesh):
    rows = ("mirror", "dp")
    in_specs = (
        P(rows, "tensor", None),
        P(None, None, "tensor"),
        P(rows, None, "tensor"),
        P(rows, None, "tensor"),
        P(rows, None, "tensor"),
        P(rows, None, "tensor"),
        P(rows, None),
    )
    out_specs = (P(rows, "tensor", None), P(rows, None, "tensor"))
    return jax.shard_map(shards, mesh=mesh, in_specs=in_specs, out_specs=out_specs, check_vma=False)
```

time: 302 us -> 67.7 us (0.22)
  waiting for transfers between devices: 239 us -> 0 us
  Pallas kernels: 0 us -> 63 us
  local copies, waits for them, and re-layouts: 28.7 us -> 3.94 us
  matrix products: 15.8 us -> 0 us
  between operations: 13.9 us -> 0.64 us
    unnamed x4 -> x0, waiting for transfers between devices: 144 us -> none
    pallas_call x0 -> x1, Pallas kernels: none -> 63 us  [shards(): pl.pallas_call(kernel, out_shape=(jax.ShapeDtypeStruct((32, 4096), BF16),...]
    reduce_scatter x1 -> x0, waiting for transfers between devices: 61.9 us -> none  [shards(): lax.psum_scatter(lax.dot_general(grad_pair, weight_flat, (((1,), (1,)), (...]
    all_gather x1 -> x0, waiting for transfers between devices: 32.9 us -> none  [shards(): gathered = lax.all_gather(layer_input, 'tensor', axis=1, tiled=True)[0]]
    unnamed x5 -> x1, local copies, waits for them, and re-layouts: 23.4 us -> 1.67 us
    dot_general x5 -> x0, matrix products: 15.3 us -> none  [the longest x1 7.19 us: shards(): lax.dot_general(gathered, grad_pair, (((0,), (0,)), ((), ())), preferred_...]
  transfers between devices with their start and end apart: 3 -> 0, of which waited for: 3 -> 0; matrix products, arithmetic and copies ran while one was open for 9% -> 0% of each run, Pallas kernels for 0% -> 0%
where the time goes in v1:
time: 67.7 us; the launch traced here: 67.6 us
  Pallas kernels  63 us (93%)
  local copies, waits for them, and re-layouts  3.94 us (6%)
    pallas_call x1, Pallas kernels, shards(): pl.pallas_call(kernel, out_shape=(jax.ShapeDtypeStruct((32, 4096), BF16),...  63 us
    reshape x1, local copies, waits for them, and re-layouts, shards(): return (input_grad.reshape(1, 32, 4096), weight_grad.reshape(128, 2, 512))  2.27 us
    unnamed x1, local copies, waits for them, and re-layouts  1.67 us

profile of v1, /device:TPU:1, one launch (start us, length us, event | category | flops | bytes accessed | tf_op | source)
XLA Modules:
  0.0 67.6 jit_solution(1918527415411716513)
XLA Ops:
  0.6 63.0 %qk_backward.1 = (bf16[32,4096]{1,0:T(8,128)(2,1)}, f32[128,1024]{1,0:T(8,128)}) custom-call(bf16[1,32,4096]{2,1,0:T(8,128)(2,1)} %x_ref.1, bf16[4096,2,512]{2,1,0:T(2,128)(2,1)} %w_hbm.1, bf16[1,256,512]{2,1,0:T(8,128)(2,1)} %q_ref.1, bf16[1,256,512]{2,1,0:T(8,128)(2,1)} %k_ref.1, bf16[1,256,512]{2,1,0:T(8,128)(2,1)} %v_ref.1, bf16[1,256,512]{2,1,0:T(8,128)(2,1)} %g_ref.1, ...), custom_call_target="tpu_custom_call" | custom-call | tf_op jit(solution)/shard_map/qk_backward/pallas_call | solution.py:399
  63.6 2.3 %reshape.11 = f32[128,2,512]{2,1,0:T(2,128)} reshape(f32[128,1024]{1,0:T(8,128)} %get-tuple-element.5) | data formatting | bytes 1048576 | tf_op jit(solution)/shard_map/reshape | solution.py:435
  65.9 1.7 %copy.12 = bf16[1,32,4096]{2,1,0:T(8,128)(2,1)} copy(bf16[1,32,4096]{2,1,0:T(8,128)(2,1)} %bitcast.1) | data formatting | bytes 524288

commit v2 on v1

--- a/solution.py
+++ b/solution.py
@@ -16,7 +16,8 @@
 TN = (((0,), (0,)), ((), ()))
 BF16 = jnp.bfloat16
 F32 = jnp.float32
-COPIES = 96
+COPIES = 112
+SLOT = {1: 1, 3: 2, 2: 3}
 
 
 def rope_tables():
@@ -35,11 +36,12 @@
 
 
 def kernel(
-    x_ref, w_hbm, q_ref, k_ref, v_ref, g_ref, doc_ref, cos_ref, sin_ref,
-    ig_ref, wg_ref,
+    x_hbm, w_hbm, q_hbm, k_hbm, v_hbm, g_hbm, doc_hbm, cos_hbm, sin_hbm,
+    ig_hbm, wg_hbm,
+    x_ref, keep_ref, q_ref, k_ref, v_ref, g_ref, doc_ref, cos_ref, sin_ref, ig_ref, wg_ref,
     w_buf, x_buf, g_buf, g_tok, p_buf, p_sib, z_out, z_one, z_two,
     t_buf, r_one, r_two, m_out, m_in,
-    w_sem, l_sem, send_sem, recv_sem,
+    l_sem, send_sem, recv_sem,
 ):
     t = lax.axis_index("tensor")
     m = lax.axis_index("mirror")
@@ -59,29 +61,47 @@
     sibling = {"tensor": zh * 2 + 1 - c}
     twin = {"mirror": 1 - m}
 
-    w_in = [
-        pltpu.make_async_copy(w_hbm.at[pl.ds(i * 512, 512)], w_buf.at[i], w_sem.at[i])
-        for i in range(8)
-    ]
-    for copy in w_in:
-        copy.start()
-    halves = (1 - m, m)
-    own_in = [
-        pltpu.make_async_copy(
-            x_ref.at[0, :, pl.ds(pl.multiple_of(halves[u] * 2048 + x * 512, 512), 512)],
-            x_buf.at[u, 0, pl.ds(pl.multiple_of(t * 32, 32), 32)],
-            l_sem.at[u],
-        )
-        for u in range(2)
-    ]
-    for copy in own_in:
-        copy.start()
-
     barrier = pltpu.get_barrier_semaphore()
     partners = [sibling, at_z(1), at_z(3), at_x(1), at_x(2), at_x(3), at_y(1), at_y(3), twin]
     for partner in partners:
         pl.semaphore_signal(barrier, inc=1, device_id=partner, device_id_type=MESH)
-    pl.semaphore_wait(barrier, len(partners))
+
+    def load(src, dst, index):
+        copy = pltpu.make_async_copy(src, dst, l_sem.at[index])
+        copy.start()
+        return copy
+
+    ready = [
+        load(q_hbm.at[0], q_ref, 0),
+        load(k_hbm.at[0], k_ref, 1),
+        load(cos_hbm, cos_ref, 2),
+        load(sin_hbm, sin_ref, 3),
+        load(g_hbm.at[0], g_ref, 4),
+        load(v_hbm.at[0], v_ref, 5),
+        load(doc_hbm, doc_ref, 6),
+    ]
+    x_in = load(x_hbm.at[0], x_ref, 25)
+    halves = (1 - m, m)
+    own_in = [
+        load(
+            x_hbm.at[0, :, pl.ds(pl.multiple_of(halves[u] * 2048 + x * 512, 512), 512)],
+            x_buf.at[u, 0, pl.ds(pl.multiple_of(t * 32, 32), 32)],
+            7 + u,
+        )
+        for u in range(2)
+    ]
+    w_in = [load(w_hbm.at[pl.ds(i * 512, 512)], w_buf.at[i], 9 + i) for i in range(8)]
+    def load_finish():
+        for copy in ready:
+            copy.wait()
+        row = lax.broadcasted_iota(jnp.int32, (SEQ, SEQ), 0)
+        col = lax.broadcasted_iota(jnp.int32, (SEQ, SEQ), 1)
+        for s in range(2):
+            docs = jnp.broadcast_to(doc_ref[:, s * SEQ : (s + 1) * SEQ].astype(F32), (SEQ, SEQ))
+            keep_ref[s] = jnp.where((col <= row) & (docs == docs.T), 1.0, 0.0)
+
+    def meet():
+        pl.semaphore_wait(barrier, len(partners))
 
     sent = []
 
@@ -99,17 +119,31 @@
         sent.append(copy)
         return copy
 
-    turned = []
-    for u in range(2):
+    turned = {}
+
+    def turn(u):
+        turned[u] = []
         for step in (1, 3, 2):
             column = pl.multiple_of(halves[u] * 2048 + lax.rem(x + step, 4) * 512, 512)
-            turned.append(
+            turned[u].append(
                 send(
-                    x_ref.at[0, :, pl.ds(column, 512)],
-                    x_buf.at[u, 4 - step, pl.ds(pl.multiple_of(t * 32, 32), 32)],
+                    x_ref.at[:, pl.ds(column, 512)],
+                    x_buf.at[u, SLOT[step], pl.ds(pl.multiple_of(t * 32, 32), 32)],
                     at_x(step),
                 )
             )
+
+    def turn_near(u):
+        turned[u][0].wait_recv()
+        turned[u][1].wait_recv()
+
+    def turn_far(u):
+        turned[u][2].wait_recv()
+
+    def own_finish():
+        x_in.wait()
+        for copy in own_in:
+            copy.wait()
 
     def piece(which, zi, half=None):
         start = (lax.rem(zi, 4) * 2 + c) * 32
@@ -117,9 +151,12 @@
             rows = pl.ds(pl.multiple_of(start, 32), 32)
         else:
             rows = pl.ds(pl.multiple_of(start + 16 * half, 16), 16)
-        if which == 0:
-            return x_buf.at[:, 0, rows]
-        return x_buf.at[which - 1, pl.ds(1, 3), rows]
+        return (
+            x_buf.at[:, 0, rows],
+            x_buf.at[0, pl.ds(1, 2), rows],
+            x_buf.at[0, 3, rows],
+            x_buf.at[1, pl.ds(1, 3), rows],
+        )[which]
 
     ring = {}
 
@@ -157,77 +194,64 @@
         for copy in ring[which, "sib"]:
             copy.wait_recv()
 
-    for copy in own_in:
-        copy.wait()
-    x_start(0)
-
-    cosine, sine = cos_ref[...], sin_ref[...]
     scale = 1.0 / math.sqrt(HD)
-    row = lax.broadcasted_iota(jnp.int32, (SEQ, SEQ), 0)
-    col = lax.broadcasted_iota(jnp.int32, (SEQ, SEQ), 1)
-    allowed = []
-    for s in range(2):
-        docs = jnp.broadcast_to(doc_ref[:, s * SEQ : (s + 1) * SEQ].astype(F32), (SEQ, SEQ))
-        allowed.append((col <= row) & (docs == docs.T))
 
     def rotate(values):
-        return values * cosine + pltpu.roll(values, 64, 1) * sine
+        return values * cos_ref[...] + pltpu.roll(values, 64, 1) * sin_ref[...]
 
     def unrotate(values):
-        return values * cosine - pltpu.roll(values, 64, 1) * sine
-
-    def heads(pair):
+        return values * cos_ref[...] - pltpu.roll(values, 64, 1) * sin_ref[...]
+
+    def head(pair, j):
+        h = 2 * pair + j
         for s in range(2):
             rows = slice(s * SEQ, (s + 1) * SEQ)
-            for j in range(2):
-                h = 2 * pair + j
-                cols = slice(h * HD, (h + 1) * HD)
-                q_rot = rotate(q_ref[0, rows, cols].astype(F32)).astype(BF16)
-                k_rot = rotate(k_ref[0, rows, cols].astype(F32)).astype(BF16)
-                scores = lax.dot_general(q_rot, k_rot, NT, preferred_element_type=F32) * scale
-                scores = jnp.where(allowed[s], scores, -1e30)
-                exps = jnp.exp(scores - jnp.max(scores, axis=-1, keepdims=True))
-                probs = exps / jnp.sum(exps, axis=-1, keepdims=True)
-                dprob = lax.dot_general(
-                    g_ref[0, rows, cols], v_ref[0, rows, cols], NT, preferred_element_type=F32
-                )
-                delta = jnp.sum(probs * dprob, axis=-1, keepdims=True)
-                dscore = (probs * (dprob - delta)).astype(BF16)
-                dq = jnp.dot(dscore, k_rot, preferred_element_type=F32) * scale
-                dk = lax.dot_general(dscore, q_rot, TN, preferred_element_type=F32) * scale
-                dq, dk = unrotate(dq), unrotate(dk)
-                g_tok[rows, h * HD : (h + 1) * HD] = dq.astype(BF16)
-                g_tok[rows, 512 + h * HD : 512 + (h + 1) * HD] = dk.astype(BF16)
-                g_buf[pair, j * 256 : j * 256 + 128, rows] = dq.T.astype(BF16)
-                g_buf[pair, j * 256 + 128 : j * 256 + 256, rows] = dk.T.astype(BF16)
+            cols = slice(h * HD, (h + 1) * HD)
+            q_rot = rotate(q_ref[rows, cols].astype(F32)).astype(BF16)
+            k_rot = rotate(k_ref[rows, cols].astype(F32)).astype(BF16)
+            scores = lax.dot_general(q_rot, k_rot, NT, preferred_element_type=F32) * scale
+            scores = jnp.where(keep_ref[s] > 0.5, scores, -1e30)
+            exps = jnp.exp(scores - jnp.max(scores, axis=-1, keepdims=True))
+            probs = exps / jnp.sum(exps, axis=-1, keepdims=True)
+            dprob = lax.dot_general(
+                g_ref[rows, cols], v_ref[rows, cols], NT, preferred_element_type=F32
+            )
+            delta = jnp.sum(probs * dprob, axis=-1, keepdims=True)
+            dscore = (probs * (dprob - delta)).astype(BF16)
+            dq = jnp.dot(dscore, k_rot, preferred_element_type=F32) * scale
+            dk = lax.dot_general(dscore, q_rot, TN, preferred_element_type=F32) * scale
+            dq, dk = unrotate(dq), unrotate(dk)
+            g_tok[rows, h * HD : (h + 1) * HD] = dq.astype(BF16)
+            g_tok[rows, 512 + h * HD : 512 + (h + 1) * HD] = dk.astype(BF16)
+            g_buf[pair, j * 256 : j * 256 + 128, rows] = dq.T.astype(BF16)
+            g_buf[pair, j * 256 + 128 : j * 256 + 256, rows] = dk.T.astype(BF16)
 
     grads = {}
 
-    def g_slot(pair, slot):
-        return g_buf.at[pair, :, pl.ds(slot * 256, 256)]
-
-    def g_start(pair):
-        grads[pair] = [
-            send(g_slot(pair, 0), g_slot(pair, 3), at_x(1)),
-            send(g_slot(pair, 0), g_slot(pair, 1), at_x(3)),
+    def g_part(h, slot, half=None):
+        row, size = (h % 2) * 256, 256
+        if half is not None:
+            row, size = row + 128 * half, 128
+        return g_buf.at[h // 2, pl.ds(row, size), pl.ds(slot * 256, 256)]
+
+    def g_start(h):
+        grads[h] = [
+            send(g_part(h, 0), g_part(h, 1), at_x(1)),
+            send(g_part(h, 0), g_part(h, 2), at_x(3)),
         ]
 
-    def g_forward(pair):
-        up, down = grads[pair]
-        low, high = pl.ds(0, 256), pl.ds(256, 256)
+    def g_forward(h):
+        up, down = grads[h]
         up.wait_recv()
-        fu = send(
-            g_buf.at[pair, low, pl.ds(768, 256)], g_buf.at[pair, low, pl.ds(512, 256)], at_x(1)
-        )
+        fu = send(g_part(h, 1, 0), g_part(h, 3, 0), at_x(1))
         down.wait_recv()
-        fd = send(
-            g_buf.at[pair, high, pl.ds(256, 256)], g_buf.at[pair, high, pl.ds(512, 256)], at_x(3)
-        )
-        grads[pair, "far"] = [fu, fd]
+        fd = send(g_part(h, 2, 1), g_part(h, 3, 1), at_x(3))
+        grads[h, "far"] = [fu, fd]
 
     def g_finish(pair):
-        for copy in grads[pair, "far"]:
-            copy.wait_recv()
+        for h in (2 * pair, 2 * pair + 1):
+            for copy in grads[h, "far"]:
+                copy.wait_recv()
 
     pick_row = lax.broadcasted_iota(jnp.int32, (256, 256), 0)
     pick_col = lax.broadcasted_iota(jnp.int32, (256, 256), 1)
@@ -285,7 +309,8 @@
         for copy in swaps[u, 2]:
             copy.wait_recv()
         total = p_sum(u, zh) + z_two[u, 0].astype(F32) + z_two[u, 1].astype(F32)
-        ig_ref[:, u * 1024 : (u + 1) * 1024] = total.astype(BF16)
+        ig_ref[u] = total.astype(BF16)
+        stored.append(load(ig_ref.at[u], ig_hbm.at[:, pl.ds(u * 1024, 1024)], 17 + u))
 
     terms = {}
 
@@ -336,75 +361,127 @@
         for j in range(2):
             for p in range(2):
                 block = total[j * 256 + p * 128 : j * 256 + p * 128 + 128]
-                at = p * 512 + (2 * pair + j) * 128
-                wg_ref[:, at : at + 128] = block.T
-
-    heads(0)
+                at = (2 * pair + j) * 128
+                wg_ref[:, p, at : at + 128] = block.T
+        span = pl.ds(pair * 256, 256)
+        stored.append(load(wg_ref.at[:, :, span], wg_hbm.at[:, :, span], 21 + pair))
+
+    stored = []
+
+    load_finish()
+    head(0, 0)
+    own_finish()
+    meet()
+    turn(0)
+    turn(1)
+    x_start(0)
     g_start(0)
-    for copy in turned:
-        copy.wait_recv()
+    head(0, 1)
+    g_start(1)
+    head(1, 0)
+    head(1, 1)
+    turn_near(0)
     x_start(1)
+    turn_far(0)
     x_start(2)
-    heads(1)
-    g_start(1)
+    x_forward(0)
     p_unit(0)
-    x_forward(0)
     p_unit(1)
+    x_forward(1)
+    g_forward(0)
     p_unit(2)
-    g_forward(0)
-    x_forward(1)
+    x_forward(2)
+    turn_near(1)
+    turn_far(1)
+    x_start(3)
+    p_one(0)
+    p_one(1)
+    g_forward(1)
+    g_start(2)
+    g_start(3)
+    p_unit(3)
     x_far(0)
-    p_unit(3)
-    x_forward(2)
-    g_forward(1)
     x_far(1)
+    x_far(2)
     x_finish(0)
     x_finish(1)
+    x_finish(2)
     g_finish(0)
     t_unit(0, 0)
-    p_one(0)
-    p_one(1)
+    g_forward(2)
+    x_forward(3)
+    p_one(2)
+    p_one(3)
     t_two(0, 0)
+    p_two(0)
+    g_forward(3)
+    p_two(1)
+    x_far(3)
     g_finish(1)
     t_unit(0, 1)
-    x_far(2)
-    p_one(2)
-    p_one(3)
-    x_finish(2)
+    x_finish(3)
     t_unit(1, 0)
     t_unit(1, 1)
-    p_two(0)
+    t_away(0)
+    p_two(2)
+    p_two(3)
     t_two(0, 1)
-    t_away(0)
-    p_two(1)
     t_two(1, 0)
+    t_two(1, 1)
     t_away(1)
-    p_two(2)
-    t_two(1, 1)
-    p_two(3)
     p_end(0)
+    p_end(1)
     t_end(0)
-    p_end(1)
+    p_end(2)
     t_end(1)
-    p_end(2)
     p_end(3)
+    for copy in stored:
+        copy.wait()
     for copy in sent:
         copy.wait_send()
 
 
+def hand_over(ig_in, wg_in, ig_out, wg_out, ig_v, wg_v, sem):
+    pairs = [(wg_in.at[pl.ds(64 * i, 64)], wg_v.at[pl.ds(64 * i, 64)]) for i in range(2)]
+    pairs.append((ig_in, ig_v))
+    outs = [wg_out.at[pl.ds(64 * i, 64)] for i in range(2)] + [ig_out.at[0]]
+    loads = [pltpu.make_async_copy(a, b, sem.at[0, i]) for i, (a, b) in enumerate(pairs)]
+    stores = [
+        pltpu.make_async_copy(pairs[i][1], out, sem.at[1, i]) for i, out in enumerate(outs)
+    ]
+    for copy in loads:
+        copy.start()
+    for i in range(3):
+        loads[i].wait()
+        stores[i].start()
+    for copy in stores:
+        copy.wait()
+
+
 def shards(layer_input, qk_weight, query_proj, key_proj, value_proj, head_grad, doc_ids):
     cosine, sine = rope_tables()
-    vmem = pl.BlockSpec(memory_space=pltpu.VMEM)
+    hbm = pl.BlockSpec(memory_space=pl.ANY)
     dma = pltpu.SemaphoreType.DMA
     input_grad, weight_grad = pl.pallas_call(
         kernel,
         out_shape=(
             jax.ShapeDtypeStruct((32, 4096), BF16),
-            jax.ShapeDtypeStruct((128, 1024), F32),
+            jax.ShapeDtypeStruct((128, 2, 512), F32),
         ),
-        in_specs=[vmem, pl.BlockSpec(memory_space=pl.ANY)] + [vmem] * 7,
-        out_specs=(vmem, vmem),
+        in_specs=[hbm] * 9,
+        out_specs=(hbm, hbm),
         scratch_shapes=[
+            pltpu.VMEM((32, 4096), BF16),
+            pltpu.VMEM((2, 128, 128), F32),
+            pltpu.VMEM((256, 512), BF16),
+            pltpu.VMEM((256, 512), BF16),
+            pltpu.VMEM((256, 512), BF16),
+            pltpu.VMEM((256, 512), BF16),
+            pltpu.VMEM((1, 256), jnp.int32),
+            pltpu.VMEM((128, 128), F32),
+            pltpu.VMEM((128, 128), F32),
+            pltpu.VMEM((4, 32, 1024), BF16),
+            pltpu.VMEM((128, 2, 512), F32),
             pltpu.VMEM((8, 512, 2, 512), BF16),
             pltpu.VMEM((2, 4, 256, 512), BF16),
             pltpu.VMEM((2, 512, 1024), BF16),
@@ -419,8 +496,7 @@
             pltpu.VMEM((4, 2, 512, 128), BF16),
             pltpu.VMEM((2, 512, 128), BF16),
             pltpu.VMEM((2, 512, 128), BF16),
-            dma((8,)),
-            dma((2,)),
+            dma((26,)),
             dma((COPIES,)),
             dma((COPIES,)),
         ],
@@ -432,7 +508,22 @@
         layer_input, qk_weight, query_proj, key_proj, value_proj, head_grad, doc_ids,
         jnp.asarray(cosine), jnp.asarray(sine),
     )
-    return (input_grad.reshape(1, 32, 4096), weight_grad.reshape(128, 2, 512))
+    return pl.pallas_call(
+        hand_over,
+        out_shape=(
+            jax.ShapeDtypeStruct((1, 32, 4096), BF16),
+            jax.ShapeDtypeStruct((128, 2, 512), F32),
+        ),
+        in_specs=[hbm] * 2,
+        out_specs=(hbm, hbm),
+        scratch_shapes=[
+            pltpu.VMEM((32, 4096), BF16),
+            pltpu.VMEM((128, 2, 512), F32),
+            dma((2, 4)),
+        ],
+        compiler_params=pltpu.CompilerParams(vmem_limit_bytes=58 << 20),
+        name="hand_over",
+    )(input_grad, weight_grad)
 
 
 def solution(mesh):

time: 67.7 us -> 58.4 us (0.86)
  Pallas kernels: 63 us -> 57.6 us
  local copies, waits for them, and re-layouts: 3.94 us -> 0 us
    pallas_call x1, Pallas kernels: 63 us -> 55.7 us  [shards(): pl.pallas_call(kernel, out_shape=(jax.ShapeDtypeStruct((32, 4096), BF16),...]
    reshape x1 -> x0, local copies, waits for them, and re-layouts: 2.27 us -> none  [shards(): return (input_grad.reshape(1, 32, 4096), weight_grad.reshape(128, 2, 512))]
    pallas_call x0 -> x1, Pallas kernels: none -> 1.9 us  [shards(): pl.pallas_call(hand_over, out_shape=(jax.ShapeDtypeStruct((1, 32, 4096),...]
    unnamed x1 -> x0, local copies, waits for them, and re-layouts: 1.67 us -> none
where the time goes in v2:
time: 58.4 us; the launch traced here: 58.3 us
  Pallas kernels  57.6 us (99%)
  between operations  0.64 us (1%)
    pallas_call x1, Pallas kernels, shards(): pl.pallas_call(kernel, out_shape=(jax.ShapeDtypeStruct((32, 4096), BF16),...  55.7 us
    pallas_call x1, Pallas kernels, shards(): pl.pallas_call(hand_over, out_shape=(jax.ShapeDtypeStruct((1, 32, 4096),...  1.9 us

profile of v2, /device:TPU:1, one launch (start us, length us, event | category | flops | bytes accessed | tf_op | source)
XLA Modules:
  0.0 58.3 jit_solution(13449856221621659209)
XLA Ops:
  0.6 55.7 %qk_backward.1 = (bf16[32,4096]{1,0:T(8,128)(2,1)}, f32[128,2,512]{2,1,0:T(2,128)}) custom-call(bf16[1,32,4096]{2,1,0:T(8,128)(2,1)} %x_hbm.1, bf16[4096,2,512]{2,1,0:T(2,128)(2,1)} %w_hbm.1, bf16[1,256,512]{2,1,0:T(8,128)(2,1)} %q_hbm.1, bf16[1,256,512]{2,1,0:T(8,128)(2,1)} %k_hbm.1, bf16[1,256,512]{2,1,0:T(8,128)(2,1)} %v_hbm.1, ...), custom_call_target="tpu_custom_call" | custom-call | tf_op jit(solution)/shard_map/qk_backward/pallas_call | solution.py:465
  56.4 1.9 %hand_over.1 = (bf16[1,32,4096]{2,1,0:T(8,128)(2,1)}, f32[128,2,512]{2,1,0:T(2,128)}) custom-call(bf16[32,4096]{1,0:T(8,128)(2,1)} %get-tuple-element.4.ig_in, f32[128,2,512]{2,1,0:T(2,128)} %get-tuple-element.5.wg_in), custom_call_target="tpu_custom_call" | custom-call | tf_op jit(solution)/shard_map/hand_over/pallas_call | solution.py:511

commit v3 on v2

--- a/solution.py
+++ b/solution.py
@@ -37,8 +37,8 @@
 
 def kernel(
     x_hbm, w_hbm, q_hbm, k_hbm, v_hbm, g_hbm, doc_hbm, cos_hbm, sin_hbm,
-    ig_hbm, wg_hbm,
-    x_ref, keep_ref, q_ref, k_ref, v_ref, g_ref, doc_ref, cos_ref, sin_ref, ig_ref, wg_ref,
+    ig_ref, wg_ref,
+    keep_ref, q_ref, k_ref, v_ref, g_ref, doc_ref, cos_ref, sin_ref,
     w_buf, x_buf, g_buf, g_tok, p_buf, p_sib, z_out, z_one, z_two,
     t_buf, r_one, r_two, m_out, m_in,
     l_sem, send_sem, recv_sem,
@@ -80,7 +80,6 @@
         load(v_hbm.at[0], v_ref, 5),
         load(doc_hbm, doc_ref, 6),
     ]
-    x_in = load(x_hbm.at[0], x_ref, 25)
     halves = (1 - m, m)
     own_in = [
         load(
@@ -127,7 +126,7 @@
             column = pl.multiple_of(halves[u] * 2048 + lax.rem(x + step, 4) * 512, 512)
             turned[u].append(
                 send(
-                    x_ref.at[:, pl.ds(column, 512)],
+                    x_hbm.at[0, :, pl.ds(column, 512)],
                     x_buf.at[u, SLOT[step], pl.ds(pl.multiple_of(t * 32, 32), 32)],
                     at_x(step),
                 )
@@ -141,7 +140,6 @@
         turned[u][2].wait_recv()
 
     def own_finish():
-        x_in.wait()
         for copy in own_in:
             copy.wait()
 
@@ -228,10 +226,9 @@
 
     grads = {}
 
-    def g_part(h, slot, half=None):
-        row, size = (h % 2) * 256, 256
-        if half is not None:
-            row, size = row + 128 * half, 128
+    def g_part(h, slot, half=0):
+        first, size = ((0, 256), (0, 96), (96, 160))[half]
+        row = (h % 2) * 256 + first
         return g_buf.at[h // 2, pl.ds(row, size), pl.ds(slot * 256, 256)]
 
     def g_start(h):
@@ -243,9 +240,9 @@
     def g_forward(h):
         up, down = grads[h]
         up.wait_recv()
-        fu = send(g_part(h, 1, 0), g_part(h, 3, 0), at_x(1))
+        fu = send(g_part(h, 1, 1), g_part(h, 3, 1), at_x(1))
         down.wait_recv()
-        fd = send(g_part(h, 2, 1), g_part(h, 3, 1), at_x(3))
+        fd = send(g_part(h, 2, 2), g_part(h, 3, 2), at_x(3))
         grads[h, "far"] = [fu, fd]
 
     def g_finish(pair):
@@ -260,24 +257,22 @@
     ).astype(BF16)
     swaps = {}
 
-    def p_unit(u):
-        for i in (2 * u, 2 * u + 1):
-            w_in[i].wait()
-            mixed = w_buf[i].reshape(1024, 512)
-            parts = [
-                jnp.dot(pick, mixed[b * 256 : (b + 1) * 256], preferred_element_type=F32).astype(
-                    BF16
-                )
-                for b in range(4)
-            ]
-            w_q = jnp.concatenate([part[:128] for part in parts], axis=0)
-            w_k = jnp.concatenate([part[128:] for part in parts], axis=0)
-            partial = lax.dot_general(
-                g_tok[:, :512], w_q, NT, preferred_element_type=F32
-            ) + lax.dot_general(g_tok[:, 512:], w_k, NT, preferred_element_type=F32)
-            off = (i % 2) * 512
-            p_buf[u, :, :, :, off : off + 512] = partial.astype(BF16).reshape(4, 2, 32, 512)
-        swaps[u] = send(p_buf.at[u, :, 1 - c], p_sib.at[u], sibling)
+    def p_half(i):
+        u, off = i // 2, (i % 2) * 512
+        w_in[i].wait()
+        mixed = w_buf[i].reshape(1024, 512)
+        parts = [
+            jnp.dot(pick, mixed[b * 256 : (b + 1) * 256], preferred_element_type=F32).astype(BF16)
+            for b in range(4)
+        ]
+        w_q = jnp.concatenate([part[:128] for part in parts], axis=0)
+        w_k = jnp.concatenate([part[128:] for part in parts], axis=0)
+        partial = lax.dot_general(
+            g_tok[:, :512], w_q, NT, preferred_element_type=F32
+        ) + lax.dot_general(g_tok[:, 512:], w_k, NT, preferred_element_type=F32)
+        p_buf[u, :, :, :, off : off + 512] = partial.astype(BF16).reshape(4, 2, 32, 512)
+        if i % 2:
+            swaps[u] = send(p_buf.at[u, :, 1 - c], p_sib.at[u], sibling)
 
     def p_sum(u, zi):
         return p_buf[u, zi, c].astype(F32) + p_sib[u, zi].astype(F32)
@@ -309,8 +304,7 @@
         for copy in swaps[u, 2]:
             copy.wait_recv()
         total = p_sum(u, zh) + z_two[u, 0].astype(F32) + z_two[u, 1].astype(F32)
-        ig_ref[u] = total.astype(BF16)
-        stored.append(load(ig_ref.at[u], ig_hbm.at[:, pl.ds(u * 1024, 1024)], 17 + u))
+        ig_ref[:, u * 1024 : (u + 1) * 1024] = total.astype(BF16)
 
     terms = {}
 
@@ -363,115 +357,107 @@
                 block = total[j * 256 + p * 128 : j * 256 + p * 128 + 128]
                 at = (2 * pair + j) * 128
                 wg_ref[:, p, at : at + 128] = block.T
-        span = pl.ds(pair * 256, 256)
-        stored.append(load(wg_ref.at[:, :, span], wg_hbm.at[:, :, span], 21 + pair))
-
-    stored = []
 
     load_finish()
     head(0, 0)
     own_finish()
     meet()
     turn(0)
+    x_start(0)
     turn(1)
-    x_start(0)
-    g_start(0)
     head(0, 1)
-    g_start(1)
     head(1, 0)
-    head(1, 1)
+    g_start(2)
     turn_near(0)
     x_start(1)
+    g_start(0)
+    head(1, 1)
+    p_half(0)
+    g_start(3)
     turn_far(0)
     x_start(2)
+    p_half(1)
     x_forward(0)
-    p_unit(0)
-    p_unit(1)
-    x_forward(1)
-    g_forward(0)
-    p_unit(2)
-    x_forward(2)
     turn_near(1)
+    p_half(2)
+    p_half(3)
     turn_far(1)
     x_start(3)
+    p_half(4)
+    g_start(1)
+    p_half(5)
+    p_half(6)
+    g_forward(2)
+    x_far(0)
+    x_forward(2)
+    x_forward(1)
+    p_one(2)
+    x_finish(0)
+    p_one(1)
+    p_half(7)
+    g_forward(3)
+    p_one(3)
+    g_forward(0)
+    x_far(2)
+    x_forward(3)
+    g_forward(1)
+    x_far(1)
+    p_two(2)
+    x_finish(1)
+    g_finish(1)
     p_one(0)
-    p_one(1)
-    g_forward(1)
-    g_start(2)
-    g_start(3)
-    p_unit(3)
-    x_far(0)
-    x_far(1)
-    x_far(2)
-    x_finish(0)
-    x_finish(1)
     x_finish(2)
+    t_unit(0, 1)
     g_finish(0)
     t_unit(0, 0)
-    g_forward(2)
-    x_forward(3)
-    p_one(2)
-    p_one(3)
+    x_far(3)
+    p_two(1)
+    t_two(0, 1)
+    p_two(3)
+    x_finish(3)
+    t_unit(1, 1)
+    t_unit(1, 0)
     t_two(0, 0)
+    p_end(2)
     p_two(0)
-    g_forward(3)
-    p_two(1)
-    x_far(3)
-    g_finish(1)
-    t_unit(0, 1)
-    x_finish(3)
-    t_unit(1, 0)
-    t_unit(1, 1)
+    t_away(1)
+    t_two(1, 1)
+    p_end(1)
+    t_two(1, 0)
     t_away(0)
-    p_two(2)
-    p_two(3)
-    t_two(0, 1)
-    t_two(1, 0)
-    t_two(1, 1)
-    t_away(1)
+    p_end(3)
     p_end(0)
-    p_end(1)
+    t_end(1)
     t_end(0)
-    p_end(2)
-    t_end(1)
-    p_end(3)
-    for copy in stored:
-        copy.wait()
     for copy in sent:
         copy.wait_send()
 
 
-def hand_over(ig_in, wg_in, ig_out, wg_out, ig_v, wg_v, sem):
-    pairs = [(wg_in.at[pl.ds(64 * i, 64)], wg_v.at[pl.ds(64 * i, 64)]) for i in range(2)]
-    pairs.append((ig_in, ig_v))
-    outs = [wg_out.at[pl.ds(64 * i, 64)] for i in range(2)] + [ig_out.at[0]]
-    loads = [pltpu.make_async_copy(a, b, sem.at[0, i]) for i, (a, b) in enumerate(pairs)]
-    stores = [
-        pltpu.make_async_copy(pairs[i][1], out, sem.at[1, i]) for i, out in enumerate(outs)
+def hand_over(ig_in, wg_in, ig_out, wg_out, sem):
+    copies = [
+        pltpu.make_async_copy(wg_in, wg_out, sem.at[0]),
+        pltpu.make_async_copy(ig_in, ig_out.at[0], sem.at[1]),
     ]
-    for copy in loads:
+    for copy in copies:
         copy.start()
-    for i in range(3):
-        loads[i].wait()
-        stores[i].start()
-    for copy in stores:
+    for copy in copies:
         copy.wait()
 
 
 def shards(layer_input, qk_weight, query_proj, key_proj, value_proj, head_grad, doc_ids):
     cosine, sine = rope_tables()
     hbm = pl.BlockSpec(memory_space=pl.ANY)
+    vmem = pl.BlockSpec(memory_space=pltpu.VMEM)
     dma = pltpu.SemaphoreType.DMA
     input_grad, weight_grad = pl.pallas_call(
         kernel,
         out_shape=(
-            jax.ShapeDtypeStruct((32, 4096), BF16),
-            jax.ShapeDtypeStruct((128, 2, 512), F32),
+            pltpu.VMEM((32, 4096), BF16),
+            pltpu.VMEM((128, 2, 512), F32),
         ),
         in_specs=[hbm] * 9,
-        out_specs=(hbm, hbm),
+        out_specs=(vmem, vmem),
         scratch_shapes=[
-            pltpu.VMEM((32, 4096), BF16),
             pltpu.VMEM((2, 128, 128), F32),
             pltpu.VMEM((256, 512), BF16),
             pltpu.VMEM((256, 512), BF16),
@@ -480,8 +466,6 @@
             pltpu.VMEM((1, 256), jnp.int32),
             pltpu.VMEM((128, 128), F32),
             pltpu.VMEM((128, 128), F32),
-            pltpu.VMEM((4, 32, 1024), BF16),
-            pltpu.VMEM((128, 2, 512), F32),
             pltpu.VMEM((8, 512, 2, 512), BF16),
             pltpu.VMEM((2, 4, 256, 512), BF16),
             pltpu.VMEM((2, 512, 1024), BF16),
@@ -496,7 +480,7 @@
             pltpu.VMEM((4, 2, 512, 128), BF16),
             pltpu.VMEM((2, 512, 128), BF16),
             pltpu.VMEM((2, 512, 128), BF16),
-            dma((26,)),
+            dma((17,)),
             dma((COPIES,)),
             dma((COPIES,)),
         ],
@@ -514,14 +498,10 @@
             jax.ShapeDtypeStruct((1, 32, 4096), BF16),
             jax.ShapeDtypeStruct((128, 2, 512), F32),
         ),
-        in_specs=[hbm] * 2,
+        in_specs=[vmem] * 2,
         out_specs=(hbm, hbm),
-        scratch_shapes=[
-            pltpu.VMEM((32, 4096), BF16),
-            pltpu.VMEM((128, 2, 512), F32),
-            dma((2, 4)),
-        ],
-        compiler_params=pltpu.CompilerParams(vmem_limit_bytes=58 << 20),
+        scratch_shapes=[dma((2,))],
+        compiler_params=pltpu.CompilerParams(vmem_limit_bytes=16 << 20),
         name="hand_over",
     )(input_grad, weight_grad)
 

time: 58.4 us -> 55.8 us (0.955)
  Pallas kernels: 57.6 us -> 55.1 us
    pallas_call x1, Pallas kernels: 55.7 us -> 54.2 us  [shards(): pl.pallas_call(kernel, out_shape=(pltpu.VMEM((32, 4096), BF16), pltpu.VME...]
    pallas_call x1, Pallas kernels: 1.9 us -> 0.89 us  [shards(): pl.pallas_call(hand_over, out_shape=(jax.ShapeDtypeStruct((1, 32, 4096),...]
where the time goes in v3:
time: 55.8 us; the launch traced here: 55.7 us
  Pallas kernels  55.1 us (99%)
  between operations  0.64 us (1%)
    pallas_call x1, Pallas kernels, shards(): pl.pallas_call(kernel, out_shape=(pltpu.VMEM((32, 4096), BF16), pltpu.VME...  54.2 us

profile of v3, /device:TPU:1, one launch (start us, length us, event | category | flops | bytes accessed | tf_op | source)
XLA Modules:
  0.0 55.7 jit_solution(16287817385633337837)
XLA Ops:
  0.6 54.2 %qk_backward.1 = (bf16[32,4096]{1,0:T(8,128)(2,1)S(1)}, f32[128,2,512]{2,1,0:T(2,128)S(1)}) custom-call(bf16[1,32,4096]{2,1,0:T(8,128)(2,1)} %x_hbm.1, bf16[4096,2,512]{2,1,0:T(2,128)(2,1)} %w_hbm.1, bf16[1,256,512]{2,1,0:T(8,128)(2,1)} %q_hbm.1, bf16[1,256,512]{2,1,0:T(8,128)(2,1)} %k_hbm.1, bf16[1,256,512]{2,1,0:T(8,128)(2,1)} %v_hbm.1, ...), custom_call_target="tpu_custom_call" | custom-call | tf_op jit(solution)/shard_map/qk_backward/pallas_call | solution.py:452
  54.8 0.9 %hand_over.1 = (bf16[1,32,4096]{2,1,0:T(8,128)(2,1)}, f32[128,2,512]{2,1,0:T(2,128)}) custom-call(bf16[32,4096]{1,0:T(8,128)(2,1)S(1)} %get-tuple-element.4.ig_in, f32[128,2,512]{2,1,0:T(2,128)S(1)} %get-tuple-element.5.wg_in), custom_call_target="tpu_custom_call" | custom-call | tf_op jit(solution)/shard_map/hand_over/pallas_call | solution.py:495

commit v4 on v3

--- a/solution.py
+++ b/solution.py
@@ -16,7 +16,7 @@
 TN = (((0,), (0,)), ((), ()))
 BF16 = jnp.bfloat16
 F32 = jnp.float32
-COPIES = 112
+COPIES = 128
 SLOT = {1: 1, 3: 2, 2: 3}
 
 
@@ -89,7 +89,7 @@
         )
         for u in range(2)
     ]
-    w_in = [load(w_hbm.at[pl.ds(i * 512, 512)], w_buf.at[i], 9 + i) for i in range(8)]
+    w_in = []
     def load_finish():
         for copy in ready:
             copy.wait()
@@ -98,6 +98,13 @@
         for s in range(2):
             docs = jnp.broadcast_to(doc_ref[:, s * SEQ : (s + 1) * SEQ].astype(F32), (SEQ, SEQ))
             keep_ref[s] = jnp.where((col <= row) & (docs == docs.T), 1.0, 0.0)
+
+    def w_start():
+        for i in range(8):
+            w_in.append(load(w_hbm.at[pl.ds(i * 512, 512)], w_buf.at[i], 9 + i))
+
+    def half(pair, j, s):
+        head(pair, j, (s,))
 
     def meet():
         pl.semaphore_wait(barrier, len(partners))
@@ -200,9 +207,9 @@
     def unrotate(values):
         return values * cos_ref[...] - pltpu.roll(values, 64, 1) * sin_ref[...]
 
-    def head(pair, j):
+    def head(pair, j, sequences=(0, 1)):
         h = 2 * pair + j
-        for s in range(2):
+        for s in sequences:
             rows = slice(s * SEQ, (s + 1) * SEQ)
             cols = slice(h * HD, (h + 1) * HD)
             q_rot = rotate(q_ref[rows, cols].astype(F32)).astype(BF16)
@@ -245,10 +252,9 @@
         fd = send(g_part(h, 2, 2), g_part(h, 3, 2), at_x(3))
         grads[h, "far"] = [fu, fd]
 
-    def g_finish(pair):
-        for h in (2 * pair, 2 * pair + 1):
-            for copy in grads[h, "far"]:
-                copy.wait_recv()
+    def g_finish(h):
+        for copy in grads[h, "far"]:
+            copy.wait_recv()
 
     pick_row = lax.broadcasted_iota(jnp.int32, (256, 256), 0)
     pick_col = lax.broadcasted_iota(jnp.int32, (256, 256), 1)
@@ -308,127 +314,139 @@
 
     terms = {}
 
-    def t_unit(u, pair):
-        term = jnp.dot(g_buf[pair], x_buf[u].reshape(1024, 512), preferred_element_type=F32)
+    def t_unit(u, h):
+        left = g_buf[h // 2, (h % 2) * 256 : (h % 2) * 256 + 256]
+        term = jnp.dot(left, x_buf[u].reshape(1024, 512), preferred_element_type=F32)
         for b in range(4):
-            t_buf[u, pair, b] = term[:, b * 128 : (b + 1) * 128].astype(BF16)
+            t_buf[u, h, b] = term[:, b * 128 : (b + 1) * 128].astype(BF16)
         far = lax.rem(y + 2, 4)
-        n = 2 * u + pair
+        n = 4 * u + h
         terms[n] = [
-            send(t_buf.at[u, pair, far, pl.ds(0, 256)], r_one.at[n, 0], at_y(1)),
-            send(t_buf.at[u, pair, far, pl.ds(256, 256)], r_one.at[n, 1], at_y(3)),
+            send(t_buf.at[u, h, far, pl.ds(0, 128)], r_one.at[n, 0], at_y(1)),
+            send(t_buf.at[u, h, far, pl.ds(128, 128)], r_one.at[n, 1], at_y(3)),
         ]
 
-    def t_two(u, pair):
-        n = 2 * u + pair
+    def t_two(u, h):
+        n = 4 * u + h
         up, down = terms[n]
         up.wait_recv()
         b = lax.rem(y + 1, 4)
-        t_buf[u, pair, b, :256] = (
-            t_buf[u, pair, b, :256].astype(F32) + r_one[n, 0].astype(F32)
+        t_buf[u, h, b, :128] = (
+            t_buf[u, h, b, :128].astype(F32) + r_one[n, 0].astype(F32)
         ).astype(BF16)
-        fu = send(t_buf.at[u, pair, b], r_two.at[n, 0], at_y(1))
+        fu = send(t_buf.at[u, h, b], r_two.at[n, 0], at_y(1))
         down.wait_recv()
         b = lax.rem(y + 3, 4)
-        t_buf[u, pair, b, 256:] = (
-            t_buf[u, pair, b, 256:].astype(F32) + r_one[n, 1].astype(F32)
+        t_buf[u, h, b, 128:] = (
+            t_buf[u, h, b, 128:].astype(F32) + r_one[n, 1].astype(F32)
         ).astype(BF16)
-        fd = send(t_buf.at[u, pair, b], r_two.at[n, 1], at_y(3))
+        fd = send(t_buf.at[u, h, b], r_two.at[n, 1], at_y(3))
         terms[n, 2] = [fu, fd]
 
-    def t_sum(u, pair):
-        n = 2 * u + pair
+    def t_sum(u, h):
+        n = 4 * u + h
         for copy in terms[n, 2]:
             copy.wait_recv()
-        return (
-            t_buf[u, pair, y].astype(F32) + r_two[n, 0].astype(F32) + r_two[n, 1].astype(F32)
-        )
-
-    def t_away(pair):
-        m_out[pair] = t_sum(0, pair).astype(BF16)
-        terms["m", pair] = send(m_out.at[pair], m_in.at[pair], twin)
-
-    def t_end(pair):
-        total = t_sum(1, pair)
-        terms["m", pair].wait_recv()
-        total = (total + m_in[pair].astype(F32)) * (1.0 / 32.0)
-        for j in range(2):
-            for p in range(2):
-                block = total[j * 256 + p * 128 : j * 256 + p * 128 + 128]
-                at = (2 * pair + j) * 128
-                wg_ref[:, p, at : at + 128] = block.T
+        return t_buf[u, h, y].astype(F32) + r_two[n, 0].astype(F32) + r_two[n, 1].astype(F32)
+
+    def t_away(h):
+        m_out[h] = t_sum(0, h).astype(BF16)
+        terms["m", h] = send(m_out.at[h], m_in.at[h], twin)
+
+    def t_end(h):
+        total = t_sum(1, h)
+        terms["m", h].wait_recv()
+        total = (total + m_in[h].astype(F32)) * (1.0 / 32.0)
+        for p in range(2):
+            wg_ref[:, p, h * 128 : h * 128 + 128] = total[p * 128 : p * 128 + 128].T
 
     load_finish()
-    head(0, 0)
+    w_start()
     own_finish()
     meet()
+    x_start(0)
     turn(0)
-    x_start(0)
     turn(1)
+    half(0, 0, 0)
+    half(0, 0, 1)
     head(0, 1)
+    g_start(0)
     head(1, 0)
-    g_start(2)
     turn_near(0)
     x_start(1)
-    g_start(0)
+    g_start(1)
     head(1, 1)
+    g_start(2)
+    g_start(3)
     p_half(0)
-    g_start(3)
     turn_far(0)
     x_start(2)
     p_half(1)
-    x_forward(0)
+    turn_far(1)
     turn_near(1)
+    x_start(3)
     p_half(2)
     p_half(3)
-    turn_far(1)
-    x_start(3)
     p_half(4)
-    g_start(1)
+    x_forward(2)
+    g_forward(0)
+    x_forward(0)
     p_half(5)
+    x_forward(1)
+    g_forward(1)
     p_half(6)
+    p_half(7)
+    p_one(0)
     g_forward(2)
+    x_forward(3)
+    p_one(3)
+    p_one(1)
+    x_far(2)
+    g_forward(3)
     x_far(0)
-    x_forward(2)
-    x_forward(1)
+    x_far(1)
+    x_finish(2)
+    g_finish(0)
     p_one(2)
     x_finish(0)
-    p_one(1)
-    p_half(7)
-    g_forward(3)
-    p_one(3)
-    g_forward(0)
-    x_far(2)
-    x_forward(3)
-    g_forward(1)
-    x_far(1)
-    p_two(2)
     x_finish(1)
+    t_unit(0, 0)
+    p_two(0)
     g_finish(1)
-    p_one(0)
-    x_finish(2)
     t_unit(0, 1)
-    g_finish(0)
-    t_unit(0, 0)
+    g_finish(3)
+    g_finish(2)
+    t_unit(0, 2)
+    t_unit(0, 3)
     x_far(3)
+    t_two(0, 0)
     p_two(1)
-    t_two(0, 1)
-    p_two(3)
     x_finish(3)
     t_unit(1, 1)
+    t_unit(1, 2)
     t_unit(1, 0)
-    t_two(0, 0)
+    p_two(3)
+    t_two(0, 2)
+    p_two(2)
+    t_two(0, 3)
+    t_unit(1, 3)
+    t_two(0, 1)
+    t_away(0)
+    t_two(1, 2)
+    t_away(2)
+    t_two(1, 1)
+    t_two(1, 0)
+    t_away(3)
+    t_two(1, 3)
+    t_away(1)
+    p_end(1)
+    t_end(0)
     p_end(2)
-    p_two(0)
-    t_away(1)
-    t_two(1, 1)
-    p_end(1)
-    t_two(1, 0)
-    t_away(0)
     p_end(3)
+    t_end(2)
     p_end(0)
+    t_end(3)
     t_end(1)
-    t_end(0)
     for copy in sent:
         copy.wait_send()
 
@@ -475,11 +493,11 @@
             pltpu.VMEM((4, 3, 32, 1024), BF16),
             pltpu.VMEM((4, 2, 16, 1024), BF16),
             pltpu.VMEM((4, 2, 32, 1024), BF16),
-            pltpu.VMEM((2, 2, 4, 512, 128), BF16),
-            pltpu.VMEM((4, 2, 256, 128), BF16),
-            pltpu.VMEM((4, 2, 512, 128), BF16),
-            pltpu.VMEM((2, 512, 128), BF16),
-            pltpu.VMEM((2, 512, 128), BF16),
+            pltpu.VMEM((2, 4, 4, 256, 128), BF16),
+            pltpu.VMEM((8, 2, 128, 128), BF16),
+            pltpu.VMEM((8, 2, 256, 128), BF16),
+            pltpu.VMEM((4, 256, 128), BF16),
+            pltpu.VMEM((4, 256, 128), BF16),
             dma((17,)),
             dma((COPIES,)),
             dma((COPIES,)),

time: 55.8 us -> 54.1 us (0.970)
  Pallas kernels: 55.1 us -> 53.3 us
    pallas_call x1, Pallas kernels: 54.2 us -> 52.4 us  [shards(): pl.pallas_call(kernel, out_shape=(pltpu.VMEM((32, 4096), BF16), pltpu.VME...]
where the time goes in v4:
time: 54.1 us; the launch traced here: 54 us
  Pallas kernels  53.3 us (99%)
  between operations  0.64 us (1%)
    pallas_call x1, Pallas kernels, shards(): pl.pallas_call(kernel, out_shape=(pltpu.VMEM((32, 4096), BF16), pltpu.VME...  52.4 us

profile of v4, /device:TPU:1, one launch (start us, length us, event | category | flops | bytes accessed | tf_op | source)
XLA Modules:
  0.0 54.0 jit_solution(4085810511904052718)
XLA Ops:
  0.6 52.4 %qk_backward.1 = (bf16[32,4096]{1,0:T(8,128)(2,1)S(1)}, f32[128,2,512]{2,1,0:T(2,128)S(1)}) custom-call(bf16[1,32,4096]{2,1,0:T(8,128)(2,1)} %x_hbm.1, bf16[4096,2,512]{2,1,0:T(2,128)(2,1)} %w_hbm.1, bf16[1,256,512]{2,1,0:T(8,128)(2,1)} %q_hbm.1, bf16[1,256,512]{2,1,0:T(8,128)(2,1)} %k_hbm.1, bf16[1,256,512]{2,1,0:T(8,128)(2,1)} %v_hbm.1, ...), custom_call_target="tpu_custom_call" | custom-call | tf_op jit(solution)/shard_map/qk_backward/pallas_call | solution.py:470
  53.1 0.9 %hand_over.1 = (bf16[1,32,4096]{2,1,0:T(8,128)(2,1)}, f32[128,2,512]{2,1,0:T(2,128)}) custom-call(bf16[32,4096]{1,0:T(8,128)(2,1)S(1)} %get-tuple-element.4.ig_in, f32[128,2,512]{2,1,0:T(2,128)S(1)} %get-tuple-element.5.wg_in), custom_call_target="tpu_custom_call" | custom-call | tf_op jit(solution)/shard_map/hand_over/pallas_call | solution.py:513

commit v5 on v4

--- a/solution.py
+++ b/solution.py
@@ -452,10 +452,13 @@
 
 
 def hand_over(ig_in, wg_in, ig_out, wg_out, sem):
-    copies = [
-        pltpu.make_async_copy(wg_in, wg_out, sem.at[0]),
-        pltpu.make_async_copy(ig_in, ig_out.at[0], sem.at[1]),
-    ]
+    copies = []
+    for i in range(4):
+        rows = pl.ds(32 * i, 32)
+        copies.append(pltpu.make_async_copy(wg_in.at[rows], wg_out.at[rows], sem.at[i]))
+    for i in range(2):
+        rows = pl.ds(16 * i, 16)
+        copies.append(pltpu.make_async_copy(ig_in.at[rows], ig_out.at[0, rows], sem.at[4 + i]))
     for copy in copies:
         copy.start()
     for copy in copies:
@@ -518,7 +521,7 @@
         ),
         in_specs=[vmem] * 2,
         out_specs=(hbm, hbm),
-        scratch_shapes=[dma((2,))],
+        scratch_shapes=[dma((6,))],
         compiler_params=pltpu.CompilerParams(vmem_limit_bytes=16 << 20),
         name="hand_over",
     )(input_grad, weight_grad)

time: 54.1 us -> 54.2 us (level)
  no operation moved by 1% of the time
where the time goes in v5:
time: 54.2 us; the launch traced here: 54 us
  Pallas kernels  53.4 us (99%)
  between operations  0.64 us (1%)
    pallas_call x1, Pallas kernels, shards(): pl.pallas_call(kernel, out_shape=(pltpu.VMEM((32, 4096), BF16), pltpu.VME...  52.4 us

profile of v5, /device:TPU:1, one launch (start us, length us, event | category | flops | bytes accessed | tf_op | source)
XLA Modules:
  0.0 54.0 jit_solution(17594030861051301058)
XLA Ops:
  0.6 52.4 %qk_backward.1 = (bf16[32,4096]{1,0:T(8,128)(2,1)S(1)}, f32[128,2,512]{2,1,0:T(2,128)S(1)}) custom-call(bf16[1,32,4096]{2,1,0:T(8,128)(2,1)} %x_hbm.1, bf16[4096,2,512]{2,1,0:T(2,128)(2,1)} %w_hbm.1, bf16[1,256,512]{2,1,0:T(8,128)(2,1)} %q_hbm.1, bf16[1,256,512]{2,1,0:T(8,128)(2,1)} %k_hbm.1, bf16[1,256,512]{2,1,0:T(8,128)(2,1)} %v_hbm.1, ...), custom_call_target="tpu_custom_call" | custom-call | tf_op jit(solution)/shard_map/qk_backward/pallas_call | solution.py:473
  53.1 0.9 %hand_over.1 = (bf16[1,32,4096]{2,1,0:T(8,128)(2,1)}, f32[128,2,512]{2,1,0:T(2,128)}) custom-call(bf16[32,4096]{1,0:T(8,128)(2,1)S(1)} %get-tuple-element.4.ig_in, f32[128,2,512]{2,1,0:T(2,128)S(1)} %get-tuple-element.5.wg_in), custom_call_target="tpu_custom_call" | custom-call | tf_op jit(solution)/shard_map/hand_over/pallas_call | solution.py:516
